TPU v7x, 32 devices: a whole 2x2x4 slice. The times are simulated.
32 devices in a mesh: shard: 4 (over x, core), ctx: 4 (over z), tp: 2 (over y).
Axes of the slice: x: 2, y: 2, z: 4, core: 2. Of those that a mesh axis runs over, the one named last changes fastest.
Arguments:
- hidden_in: bfloat16 [4096, 2048], P(('shard', 'ctx')), may hold values from -6 to 6
- gain_attn: bfloat16 [2048], P(('shard', 'ctx')), may hold values from 0.5 to 1.5
- w_qkv: bfloat16 [3, 2048, 2048], P(None, ('shard', 'ctx'), 'tp'), may hold values from -1 to 1
- w_out: bfloat16 [2048, 2048], P('tp', ('shard', 'ctx')), may hold values from -0.5 to 0.5
- gain_mlp: bfloat16 [2048], P(('shard', 'ctx')), may hold values from 0.5 to 1.5
- w_gate_up: bfloat16 [2, 2048, 8192], P(None, ('shard', 'ctx'), 'tp'), may hold values from -0.125 to 0.125
- w_down: bfloat16 [8192, 2048], P('tp', ('shard', 'ctx')), may hold values from -0.0625 to 0.0625
- segments: int32 [4, 1024], P('shard'), may hold values from 0 to 3, never falling along the last dimension, each value on 1 to 512 neighbouring positions
- cotangent: bfloat16 [4096, 2048], P(('shard', 'ctx')), may hold values from -6 to 6
Outputs:
- block_out: bfloat16 [4096, 2048], P(('shard', 'ctx'))
- grad_input: float32 [4096, 2048], P(('shard', 'ctx'))
- grad_gain_attn: float32 [2048], P(('shard', 'ctx'))
- grad_w_qkv: float32 [3, 2048, 2048], P(None, ('shard', 'ctx'), 'tp')
- grad_w_out: float32 [2048, 2048], P('tp', ('shard', 'ctx'))
- grad_gain_mlp: float32 [2048], P(('shard', 'ctx'))
- grad_w_gate_up: float32 [2, 2048, 8192], P(None, ('shard', 'ctx'), 'tp')
- grad_w_down: float32 [8192, 2048], P('tp', ('shard', 'ctx'))
Inputs may be any that keep to these rules, and one draw needn't show every extreme that they name: `segments`: each row holds one group's 1024 segment numbers; they never fall, and each segment covers 1 to 512 positions, one exactly 512.
All inputs are finite; a program needn't handle non-finite values.
Results may differ from a plain program's by a relative error of at most 0.025.
Values may be sent and summed in bfloat16 or wider, within the bound.
No kernel may reach another device: no remote copies, remote signals or barrier semaphores. Data moves between devices by JAX's collectives and lax.ppermute only.
A program may use at most 256 MiB of HBM per device.

v0:
```python
import jax
import jax.numpy as jnp
from jax import lax
from jax.sharding import PartitionSpec as P

HD = 64
EPSILON = 1e-05
ROPE_BASE = 130000.0
MASKED = -1e30


def contract(form, left_in, right_in):
    return jnp.einsum(form, left_in, right_in, preferred_element_type=jnp.float32)


def positions_of(seg_row):
    length_all = seg_row.shape[0]
    index_all = jnp.arange(length_all, dtype=jnp.int32)
    starts = jnp.concatenate([jnp.ones((1,), dtype=jnp.bool_), seg_row[1:] != seg_row[:-1]])
    first_index = lax.cummax(jnp.where(starts, index_all, jnp.zeros_like(index_all)), axis=0)
    return index_all - first_index


def rope_tables(positions, head_size):
    half_size = head_size // 2
    frequency = ROPE_BASE ** (-(jnp.arange(half_size, dtype=jnp.float32) * (2.0 / head_size)))
    angles = positions.astype(jnp.float32)[:, None] * frequency[None, :]
    return (jnp.cos(angles), jnp.sin(angles))


def rotate_heads(values_in, cosine_table, sine_table, head_size):
    rows_count = values_in.shape[0]
    shaped = values_in.reshape(rows_count, -1, head_size)
    half_size = head_size // 2
    first_half = shaped[..., :half_size]
    second_half = shaped[..., half_size:]
    cosine_rows = cosine_table[:, None, :]
    sine_rows = sine_table[:, None, :]
    turned = jnp.concatenate(
        [
            first_half * cosine_rows - second_half * sine_rows,
            second_half * cosine_rows + first_half * sine_rows,
        ],
        -1,
    )
    return turned.reshape(rows_count, -1)


def block_layout(array_in, block_rows):
    blocks_count = array_in.shape[0] // block_rows
    return array_in.reshape((blocks_count, block_rows) + array_in.shape[1:])


def with_previous(blocks, fill_value):
    earlier = jnp.concatenate([jnp.full_like(blocks[:1], fill_value), blocks[:-1]], 0)
    return jnp.concatenate([earlier, blocks], 1)


def block_masks(seg_row, block_rows):
    index_all = jnp.arange(seg_row.shape[0], dtype=jnp.int32)
    seg_query = block_layout(seg_row, block_rows)
    index_query = block_layout(index_all, block_rows)
    return (seg_query, index_query, with_previous(seg_query, -1), with_previous(index_query, 0))


def heads_view(array_in, head_size):
    return array_in.reshape(array_in.shape[0], -1, head_size)


def block_scores(
    query_blk, key_blk, seg_query_blk, index_query_blk, seg_key_blk, index_key_blk, head_size
):
    allowed = (seg_key_blk[None, :] == seg_query_blk[:, None]) & (
        index_key_blk[None, :] <= index_query_blk[:, None]
    )
    scores = contract("qhd,khd->hqk", query_blk, key_blk) * head_size ** (-0.5)
    return jnp.where(allowed[None], scores, MASKED)


def attention_forward(queries, keys_rot, value_vecs, seg_row, head_size):
    group_rows = queries.shape[0]
    block_rows = min(512, group_rows)
    query_blocks = block_layout(heads_view(queries, head_size), block_rows)
    key_blocks = with_previous(block_layout(heads_view(keys_rot, head_size), block_rows), 0)
    value_blocks = with_previous(block_layout(heads_view(value_vecs, head_size), block_rows), 0)
    seg_query, index_query, seg_keys, index_keys = block_masks(seg_row, block_rows)

    def one_block(block_items):
        query_blk, key_blk, value_blk, seg_qb, index_qb, seg_kb, index_kb = block_items
        scores = block_scores(query_blk, key_blk, seg_qb, index_qb, seg_kb, index_kb, head_size)
        row_max = jnp.max(scores, -1, keepdims=True)
        log_total = row_max + jnp.log(jnp.sum(jnp.exp(scores - row_max), -1, keepdims=True))
        weights_low = jnp.exp(scores - log_total).astype(jnp.bfloat16)
        block_result = contract("hqk,khd->qhd", weights_low, value_blk)
        return (block_result.astype(jnp.bfloat16).reshape(block_rows, -1), log_total[..., 0])

    result_blocks, log_blocks = lax.map(
        one_block,
        (query_blocks, key_blocks, value_blocks, seg_query, index_query, seg_keys, index_keys),
    )
    return (result_blocks.reshape(group_rows, -1), log_blocks)


def attention_backward(
    queries, keys_rot, value_vecs, attn, grad_attn, log_blocks, seg_row, head_size
):
    group_rows = queries.shape[0]
    block_rows = min(512, group_rows)
    score_scale = head_size ** (-0.5)
    query_blocks = block_layout(heads_view(queries, head_size), block_rows)
    key_blocks = with_previous(block_layout(heads_view(keys_rot, head_size), block_rows), 0)
    value_blocks = with_previous(block_layout(heads_view(value_vecs, head_size), block_rows), 0)
    attn_blocks = block_layout(heads_view(attn, head_size), block_rows)
    grad_blocks = block_layout(heads_view(grad_attn, head_size), block_rows)
    seg_query, index_query, seg_keys, index_keys = block_masks(seg_row, block_rows)

    def one_block(block_items):
        (
            query_blk,
            key_blk,
            value_blk,
            attn_blk,
            grad_blk,
            log_blk,
            seg_qb,
            index_qb,
            seg_kb,
            index_kb,
        ) = block_items
        scores = block_scores(query_blk, key_blk, seg_qb, index_qb, seg_kb, index_kb, head_size)
        probs = jnp.exp(scores - log_blk[..., None])
        probs_low = probs.astype(jnp.bfloat16)
        grad_value_blk = contract("hqk,qhd->khd", probs_low, grad_blk)
        grad_probs = contract("qhd,khd->hqk", grad_blk, value_blk)
        diag = jnp.sum(grad_blk.astype(jnp.float32) * attn_blk.astype(jnp.float32), -1).T
        grad_scores = (probs * (grad_probs - diag[..., None])).astype(jnp.bfloat16)
        grad_query_blk = contract("hqk,khd->qhd", grad_scores, key_blk) * score_scale
        grad_key_blk = contract("hqk,qhd->khd", grad_scores, query_blk) * score_scale
        return (grad_query_blk, grad_key_blk, grad_value_blk)

    grad_query_b, grad_key_b, grad_value_b = lax.map(
        one_block,
        (
            query_blocks,
            key_blocks,
            value_blocks,
            attn_blocks,
            grad_blocks,
            log_blocks,
            seg_query,
            index_query,
            seg_keys,
            index_keys,
        ),
    )

    def fold_pairs(pairs):
        earlier = pairs[:, :block_rows]
        current = pairs[:, block_rows:]
        shifted = jnp.concatenate([earlier[1:], jnp.zeros_like(earlier[:1])], 0)
        return (current + shifted).reshape(group_rows, -1).astype(jnp.bfloat16)

    return (
        grad_query_b.reshape(group_rows, -1).astype(jnp.bfloat16),
        fold_pairs(grad_key_b),
        fold_pairs(grad_value_b),
    )


def on_device(hidden_in, gain_attn, w_qkv, w_out, gain_mlp, w_gate_up, w_down, segments, cotangent):
    token_rows = hidden_in.shape[0]
    seg_row = segments[0]
    positions = lax.dynamic_slice_in_dim(
        positions_of(seg_row), lax.axis_index("ctx") * token_rows, token_rows
    )
    cosine_table, sine_table = rope_tables(positions, HD)
    gathered = (
        lax.all_gather(gain_attn, ("shard", "ctx"), axis=0, tiled=True),
        lax.all_gather(w_qkv, ("shard", "ctx"), axis=1, tiled=True),
        lax.all_gather(w_out, ("shard", "ctx"), axis=1, tiled=True),
        lax.all_gather(gain_mlp, ("shard", "ctx"), axis=0, tiled=True),
        lax.all_gather(w_gate_up, ("shard", "ctx"), axis=1, tiled=True),
        lax.all_gather(w_down, ("shard", "ctx"), axis=1, tiled=True),
    )
    gain_full_one, qkv_full, out_full, gain_full_two, gate_up_full, down_full = gathered
    resid_in = hidden_in.astype(jnp.float32)
    scale_one = lax.rsqrt(jnp.mean(resid_in * resid_in, -1, keepdims=True) + EPSILON)
    gain_one = gain_full_one.astype(jnp.float32)
    normed_one = (resid_in * scale_one * gain_one).astype(jnp.bfloat16)
    projected = contract("td,jdc->jtc", normed_one, qkv_full)
    queries = rotate_heads(projected[0], cosine_table, sine_table, HD).astype(jnp.bfloat16)
    keys_rot = rotate_heads(projected[1], cosine_table, sine_table, HD).astype(jnp.bfloat16)
    value_vecs = projected[2].astype(jnp.bfloat16)
    query_heads, key_heads, value_heads = (
        lax.all_to_all(queries, "ctx", split_axis=1, concat_axis=0, tiled=True),
        lax.all_to_all(keys_rot, "ctx", split_axis=1, concat_axis=0, tiled=True),
        lax.all_to_all(value_vecs, "ctx", split_axis=1, concat_axis=0, tiled=True),
    )
    attn_heads, log_blocks = attention_forward(query_heads, key_heads, value_heads, seg_row, HD)
    attn_tokens = lax.all_to_all(attn_heads, "ctx", split_axis=0, concat_axis=1, tiled=True)
    attn_terms = jnp.dot(attn_tokens, out_full, preferred_element_type=jnp.float32)
    gain_two = gain_full_two.astype(jnp.float32)
    resid_mid = resid_in + lax.psum(attn_terms.astype(jnp.bfloat16), "tp").astype(jnp.float32)
    scale_two = lax.rsqrt(jnp.mean(resid_mid * resid_mid, -1, keepdims=True) + EPSILON)
    normed_two = (resid_mid * scale_two * gain_two).astype(jnp.bfloat16)
    gate_up = contract("td,jdf->jtf", normed_two, gate_up_full)
    gate_proj = gate_up[0]
    up_proj = gate_up[1]
    sigmoid_gate = jax.nn.sigmoid(gate_proj)
    activated = (gate_proj * sigmoid_gate * up_proj).astype(jnp.bfloat16)
    mlp_terms = jnp.dot(activated, down_full, preferred_element_type=jnp.float32)
    block_out = (
        resid_mid + lax.psum(mlp_terms.astype(jnp.bfloat16), "tp").astype(jnp.float32)
    ).astype(jnp.bfloat16)
    again = (
        lax.all_gather(w_qkv, ("shard", "ctx"), axis=1, tiled=True),
        lax.all_gather(w_out, ("shard", "ctx"), axis=1, tiled=True),
        lax.all_gather(w_gate_up, ("shard", "ctx"), axis=1, tiled=True),
        lax.all_gather(w_down, ("shard", "ctx"), axis=1, tiled=True),
    )
    qkv_back, out_back, gate_up_back, down_back = again
    grad_act = contract("td,fd->tf", cotangent, down_back)
    grad_w_down = contract("tf,td->fd", activated, cotangent)
    grad_gate = grad_act * up_proj * sigmoid_gate * (1.0 + gate_proj * (1.0 - sigmoid_gate))
    grad_up = grad_act * gate_proj * sigmoid_gate
    grad_pair = jnp.stack([grad_gate, grad_up]).astype(jnp.bfloat16)
    grad_w_gate_up = contract("td,jtf->jdf", normed_two, grad_pair)
    terms_two = contract("jtf,jdf->td", grad_pair, gate_up_back)
    grad_normed_two = lax.psum(terms_two.astype(jnp.bfloat16), "tp").astype(jnp.float32)
    cot_rows = cotangent.astype(jnp.float32)
    grad_gain_mlp = jnp.sum(grad_normed_two * resid_mid * scale_two, 0)
    scaled_two = grad_normed_two * gain_two
    grad_mid = (
        cot_rows
        + scale_two * scaled_two
        - resid_mid * scale_two**3 * jnp.mean(scaled_two * resid_mid, -1, keepdims=True)
    )
    grad_mid_low = grad_mid.astype(jnp.bfloat16)
    grad_w_out = contract("tc,td->cd", attn_tokens, grad_mid_low)
    grad_attn_tokens = contract("td,cd->tc", grad_mid_low, out_back).astype(jnp.bfloat16)
    grad_attn_heads = lax.all_to_all(
        grad_attn_tokens, "ctx", split_axis=1, concat_axis=0, tiled=True
    )
    grad_query_heads, grad_key_heads, grad_value_heads = attention_backward(
        query_heads, key_heads, value_heads, attn_heads, grad_attn_heads, log_blocks, seg_row, HD
    )
    grad_queries, grad_keys, grad_values = (
        lax.all_to_all(grad_query_heads, "ctx", split_axis=0, concat_axis=1, tiled=True),
        lax.all_to_all(grad_key_heads, "ctx", split_axis=0, concat_axis=1, tiled=True),
        lax.all_to_all(grad_value_heads, "ctx", split_axis=0, concat_axis=1, tiled=True),
    )
    pre_query = rotate_heads(
        grad_queries.astype(jnp.float32), cosine_table, -sine_table, HD
    ).astype(jnp.bfloat16)
    pre_key = rotate_heads(grad_keys.astype(jnp.float32), cosine_table, -sine_table, HD).astype(
        jnp.bfloat16
    )
    grad_proj = jnp.stack([pre_query, pre_key, grad_values])
    grad_w_qkv = contract("td,jtc->jdc", normed_one, grad_proj)
    terms_one = contract("jtc,jdc->td", grad_proj, qkv_back)
    grad_normed_one = lax.psum(terms_one.astype(jnp.bfloat16), "tp").astype(jnp.float32)
    grad_gain_attn = jnp.sum(grad_normed_one * resid_in * scale_one, 0)
    scaled_one = grad_normed_one * gain_one
    grad_input = (
        grad_mid
        + scale_one * scaled_one
        - resid_in * scale_one**3 * jnp.mean(scaled_one * resid_in, -1, keepdims=True)
    )
    owned = (
        lax.psum_scatter(
            grad_gain_attn.astype(jnp.bfloat16), ("shard", "ctx"), scatter_dimension=0, tiled=True
        ).astype(jnp.float32),
        lax.psum_scatter(
            grad_w_qkv.astype(jnp.bfloat16), ("shard", "ctx"), scatter_dimension=1, tiled=True
        ).astype(jnp.float32),
        lax.psum_scatter(
            grad_w_out.astype(jnp.bfloat16), ("shard", "ctx"), scatter_dimension=1, tiled=True
        ).astype(jnp.float32),
        lax.psum_scatter(
            grad_gain_mlp.astype(jnp.bfloat16), ("shard", "ctx"), scatter_dimension=0, tiled=True
        ).astype(jnp.float32),
        lax.psum_scatter(
            grad_w_gate_up.astype(jnp.bfloat16), ("shard", "ctx"), scatter_dimension=1, tiled=True
        ).astype(jnp.float32),
        lax.psum_scatter(
            grad_w_down.astype(jnp.bfloat16), ("shard", "ctx"), scatter_dimension=1, tiled=True
        ).astype(jnp.float32),
    )
    return (block_out, grad_input, owned[0], owned[1], owned[2], owned[3], owned[4], owned[5])


def solution(mesh):
    placed = (
        P(("shard", "ctx"), None),
        P(("shard", "ctx")),
        P(None, ("shard", "ctx"), "tp"),
        P("tp", ("shard", "ctx")),
        P(("shard", "ctx")),
        P(None, ("shard", "ctx"), "tp"),
        P("tp", ("shard", "ctx")),
        P("shard", None),
        P(("shard", "ctx"), None),
    )
    return jax.shard_map(
        on_device,
        mesh=mesh,
        in_specs=placed,
        out_specs=(
            P(("shard", "ctx"), None),
            P(("shard", "ctx"), None),
            P(("shard", "ctx")),
            P(None, ("shard", "ctx"), "tp"),
            P("tp", ("shard", "ctx")),
            P(("shard", "ctx")),
            P(None, ("shard", "ctx"), "tp"),
            P("tp", ("shard", "ctx")),
        ),
        check_vma=False,
    )
```

profile of v0, /device:TPU:0, one launch (start us, length us, event | category | flops | bytes accessed | tf_op | source)
XLA Modules:
  0.0 1597.4 jit_solution(17848206042767868809)
XLA Ops:
  8.7 35.0 %all-gather = bf16[16,1,128]{2,1,0:T(2,128)(2,1)S(1)} all-gather(bf16[1,1,128]{2,1,0:T(2,128)(2,1)} %bitcast.306), channel_id=1, replica_groups=mesh['shard'=4,'ctx'=4,'tp'=2] {'shard','ctx'}, dimensions={0}, use_global_device_ids=true | all-gather | bytes 4352 | tf_op jit(solution)/shard_map/all_gather | solution.py:178
  46.6 66.9 %all-gather.7.cloned.1.call-done = bf16[3,2048,1024]{2,1,0:T(8,128)(2,1)} async-done(((bf16[3,128,1024]{2,1,0:T(8,128)(2,1)}), bf16[3,2048,1024]{2,1,0:T(8,128)(2,1)}) %all-gather.7.cloned.1.call-update) | async-done | bytes 12582928 | tf_op jit(solution)/shard_map/all_gather | solution.py:179
  113.5 6.5 convolution_bitcast_fusion.3
  134.2 13.5 all-to-all-done
  152.1 26.5 %all-to-all-done.2 = bf16[256,4,256]{0,2,1:T(8,128)(2,1)S(1)} async-done(((bf16[256,4,256]{0,2,1:T(8,128)(2,1)}), bf16[256,4,256]{0,2,1:T(8,128)(2,1)S(1)}, u32[]{:S(2)}, u32[]{:S(2)}) %all-to-all-start.2) | async-done | bytes 524320 | tf_op jit(solution)/shard_map/all_to_all | solution.py:196
  200.5 14.2 while.26
  215.7 18.5 %all_to_all.107 = bf16[4,256,256]{2,1,0:T(8,128)(2,1)} all-to-all(bf16[4,256,256]{2,1,0:T(8,128)(2,1)} %bitcast.284), channel_id=1, replica_groups=mesh['shard'=4,'ctx'=4,'tp'=2] {'ctx'}, dimensions={0} | all-to-all | bytes 1048576 | tf_op jit(solution)/shard_map/all_to_all | solution.py:200
  242.1 28.8 %all-gather.1 = bf16[16,1,128]{2,1,0:T(2,128)(2,1)S(1)} all-gather(bf16[1,1,128]{2,1,0:T(2,128)(2,1)S(1)} %bitcast.307), channel_id=1, replica_groups=mesh['shard'=4,'ctx'=4,'tp'=2] {'shard','ctx'}, dimensions={0}, use_global_device_ids=true | all-gather | bytes 4352 | tf_op jit(solution)/shard_map/all_gather | solution.py:181
  270.9 8.4 all-reduce.14.cloned.1.call-done
  281.0 177.7 %all-gather.11.cloned.1.call-done = bf16[2,2048,4096]{2,1,0:T(8,128)(2,1)} async-done(((bf16[2,128,4096]{2,1,0:T(8,128)(2,1)}), bf16[2,2048,4096]{2,1,0:T(8,128)(2,1)}) %all-gather.11.cloned.1.call-update) | async-done | bytes 33554448 | tf_op jit(solution)/shard_map/all_gather | solution.py:182
  458.6 18.2 %convolution_bitcast_fusion = f32[2,256,4096]{2,1,0:T(8,128)} fusion(bf16[2,2048,4096]{2,1,0:T(8,128)(2,1)} %all-gather.11.cloned.1.call-done, bf16[256,2048]{1,0:T(8,128)(2,1)} %all-reduce.14.cloned.1.call-done, bf16[256,2048]{1,0:T(8,128)(2,1)S(1)} %copy-done, f32[2048]{0:T(1024)S(1)} %bitcast.300, f32[256]{0:T(256)S(1)} %get-tuple-element.337), kind=kOutput, calls=%fused_computation.72 | convolution fusion | flops 8593080320 | bytes 44049408 | tf_op jit(solution)/shard_map/td,jdf->jtf/dot_general | solution.py:13
  476.8 113.6 %all-gather.13.cloned.1.call-done = bf16[4096,2048]{1,0:T(8,128)(2,1)} async-done(((bf16[4096,128]{1,0:T(8,128)(2,1)}), bf16[4096,2048]{1,0:T(8,128)(2,1)}) %all-gather.13.cloned.1.call-update) | async-done | bytes 16777232 | tf_op jit(solution)/shard_map/all_gather | solution.py:183
  590.4 13.4 fusion.74
  603.8 16.7 %fusion.52 = bf16[256,2048]{1,0:T(8,128)(2,1)} fusion(bf16[2,2048,4096]{2,1,0:T(8,128)(2,1)} %all-gather.11.cloned.1.call-done, bf16[1,256,4096]{2,1,0:T(8,128)(2,1)} %get-tuple-element.313, bf16[1,256,4096]{2,1,0:T(8,128)(2,1)} %get-tuple-element.312), kind=kOutput, calls=%fused_computation.92 | convolution fusion | flops 8592556032 | bytes 38797312 | tf_op jit(solution)/shard_map/jtf,jdf->td/dot_general | solution.py:13
  620.5 38.4 %all-reduce.16.cloned.1.call-done = bf16[256,2048]{1,0:T(8,128)(2,1)} async-done(((bf16[256,2048]{1,0:T(8,128)(2,1)}), bf16[256,2048]{1,0:T(8,128)(2,1)}) %all-reduce.16.cloned.1.call-update) | async-done | bytes 1048592 | tf_op jit(solution)/shard_map/psum | solution.py:229
  671.7 14.3 all-to-all-done.4
  691.0 24.8 %while.27 = (s32[]{:T(128)}, bf16[2,512,4,64]{1,3,2,0:T(8,128)(2,1)}, f32[2,1024,4,64]{1,3,2,0:T(8,128)}, f32[2,1024,4,64]{1,3,2,0:T(8,128)}, bf16[2,1024,4,64]{...) while((s32[]{:T(128)}, ...), condition=%wide.region_14.15_spmd, body=%wide.region_12.14_spmd.sunk | while | flops 1365637120 | bytes 89220488 | solution.py:141
  724.9 12.4 all-to-all-done.7
  760.2 9.2 convolution_convert_fusion.2
  777.6 9.0 fusion.53
  793.1 6.4 copy.113
  800.2 7.9 convert_bitcast_fusion.1
  808.1 27.7 %copy.111 = bf16[3,2048,1024]{2,0,1:T(4,128)(2,1)} copy(bf16[3,2048,1024]{1,2,0:T(8,128)(2,1)} %convert_bitcast_fusion.1) | data formatting | bytes 25165824
  835.8 15.8 copy.119
  851.7 10.1 convolution_convert_fusion
  861.8 21.6 %copy.117 = bf16[4096,2048]{0,1:T(8,128)(2,1)} copy(bf16[4096,2048]{1,0:T(8,128)(2,1)} %convolution_convert_fusion) | data formatting | bytes 33554432
  883.7 16.4 %convert_bitcast_fusion = bf16[2,2048,4096]{1,2,0:T(8,128)(2,1)} fusion(bf16[1,256,4096]{2,1,0:T(8,128)(2,1)} %get-tuple-element.313, bf16[1,256,4096]{2,1,0:T(8,128)(2,1)} %get-tuple-element.312, bf16[256,2048]{1,0:T(8,128)(2,1)S(1)} %copy-done.3, bf16[256,2048]{1,0:T(8,128)(2,1)S(1)} %copy-done, f32[2048]{0:T(1024)S(1)} %bitcast.304, ...), kind=kOutput, calls=%fused_computation.69 | convolution fusion | flops 8611954688 | bytes 39855104 | tf_op jit(solution)/shard_map/td,jtf->jdf/dot_general | solution.py:13
  900.1 83.3 %copy.115 = bf16[2,2048,4096]{2,0,1:T(2,128)(2,1)} copy(bf16[2,2048,4096]{1,2,0:T(8,128)(2,1)} %convert_bitcast_fusion) | data formatting | bytes 67108864
  983.5 29.6 %copy.120 = bf16[256,8,2,4096]{3,1,2,0:T(8,128)(2,1)} copy(bf16[256,8,2,4096]{3,2,1,0:T(2,128)(2,1)} %bitcast.260) | data formatting | bytes 67108864
  1016.8 33.2 %all-reduce.8 = (bf16[2048]{0:T(1024)(128)(2,1)S(1)}, bf16[2048]{0:T(1024)(128)(2,1)S(1)}) all-reduce(bf16[2048]{0:T(1024)(128)(2,1)S(1)} %get-tuple-element.246, bf16[2048]{0:T(1024)(128)(2,1)S(1)} %copy-done.32), channel_id=2, replica_groups=mesh['shard'=4,'ctx'=4,'tp'=2] {'shard','ctx'}, use_global_device_ids=true, to_apply=%region_18.19.clone | all-reduce | flops 4096 | bytes 16384
  1068.6 175.6 %reduce-scatter.19.cloned.1.call-done = bf16[128,4096]{1,0:T(8,128)(2,1)} async-done(((bf16[2048,4096]{1,0:T(8,128)(2,1)}), bf16[128,4096]{1,0:T(8,128)(2,1)}) %reduce-scatter.19.cloned.1.call-update) | async-done | bytes 1048592
  1247.2 330.9 %reduce-scatter.17.cloned.1.call-done = bf16[128,8192]{1,0:T(8,128)(2,1)} async-done(((bf16[2048,8192]{1,0:T(8,128)(2,1)}), bf16[128,8192]{1,0:T(8,128)(2,1)}) %reduce-scatter.17.cloned.1.call-update) | async-done | bytes 2097168
  (263 shorter events, 196.1 us)
Async XLA Ops:
  7.2 106.4 %copy-start = (bf16[256,2048]{1,0:T(8,128)(2,1)S(1)}, bf16[256,2048]{1,0:T(8,128)(2,1)}, u32[]{:S(2)}) copy-start(bf16[256,2048]{1,0:T(8,128)(2,1)} %param.13) | copy-start | bytes 3145732
  7.2 38.6 %copy-start.29 = (s32[1,1024]{1,0:T(1,128)S(1)}, s32[1,1024]{1,0:T(1,128)}, u32[]{:S(2)}) copy-start(s32[1,1024]{1,0:T(1,128)} %param.20) | copy-start | bytes 12292
  7.2 106.3 %all-gather.7.cloned.1.call-start = ((), (), s32[]{:S(2)}) async-start(), calls=%async_computation.12 | async-start | bytes 13369344 | tf_op jit(solution)/shard_map/all_gather | solution.py:179
  7.9 228.3 %all-gather.9.cloned.1.call-start = ((), (), s32[]{:S(2)}) async-start(), calls=%async_computation.13 | async-start | bytes 4456448 | tf_op jit(solution)/shard_map/all_gather | solution.py:180
  43.7 69.9 %copy-start.24 = (f32[16,1,128]{2,1,0:T(1,128)}, f32[16,1,128]{2,1,0:T(1,128)S(1)}, u32[]{:S(2)}) copy-start(f32[16,1,128]{2,1,0:T(1,128)S(1)} %convert_element_type.257) | copy-start | bytes 24580
  45.8 67.8 %copy-start.30 = (f32[256]{0:T(256)}, f32[256]{0:T(256)S(1)}, u32[]{:S(2)}) copy-start(f32[256]{0:T(256)S(1)} %get-tuple-element.335) | copy-start | bytes 3076
  122.8 25.0 %all-to-all-start = ((bf16[256,4,256]{0,2,1:T(8,128)(2,1)}), bf16[256,4,256]{0,2,1:T(8,128)(2,1)}, u32[]{:S(2)}, u32[]{:S(2)}) async-start(bf16[256,4,256]{0,2,1:T(8,128)(2,1)} %bitcast.31), calls=%async_computation | async-start | bytes 1048576 | tf_op jit(solution)/shard_map/all_to_all | solution.py:197
  133.4 17.9 %copy-start.17 = (bf16[256,16,32]{0,2,1:T(8,128)(2,1)S(1)}, bf16[256,16,32]{0,2,1:T(8,128)(2,1)}, u32[]{:S(2)}) copy-start(bf16[256,16,32]{0,2,1:T(8,128)(2,1)} %get-tuple-element.330) | copy-start | bytes 786436
  133.4 50.4 %slice-start = ((s32[1,1024]{1,0:T(1,128)}), s32[1,512]{1,0:T(1,128)S(1)}, s32[]{:S(2)}) async-start(s32[1,1024]{1,0:T(1,128)} %param.20), calls=%async_computation.23 | async-start | bytes 4096 | tf_op jit(solution)/shard_map/slice | solution.py:55
  147.8 30.8 %all-to-all-start.2 = ((bf16[256,4,256]{0,2,1:T(8,128)(2,1)}), bf16[256,4,256]{0,2,1:T(8,128)(2,1)S(1)}, u32[]{:S(2)}, u32[]{:S(2)}) async-start(bf16[256,4,256]{0,2,1:T(8,128)(2,1)} %bitcast.39), calls=%async_computation.2 | async-start | bytes 1048576 | tf_op jit(solution)/shard_map/all_to_all | solution.py:196
  178.6 18.6 %all-to-all-start.1 = ((bf16[256,4,256]{0,2,1:T(8,128)(2,1)}), bf16[256,4,256]{0,2,1:T(8,128)(2,1)S(1)}, u32[]{:S(2)}, u32[]{:S(2)}) async-start(bf16[256,4,256]{0,2,1:T(8,128)(2,1)} %bitcast.36), calls=%async_computation.1 | async-start | bytes 1048576 | tf_op jit(solution)/shard_map/all_to_all | solution.py:195
  182.0 97.3 %all-reduce.14.cloned.1.call-start = ((), (), s32[]{:S(2)}) async-start(), calls=%async_computation.14 | async-start | bytes 2097152 | tf_op jit(solution)/shard_map/psum | solution.py:203
  214.7 26.2 %copy-start.7 = (bf16[2,512,256]{1,2,0:T(8,128)(2,1)}, bf16[2,512,256]{1,2,0:T(8,128)(2,1)S(1)}, u32[]{:S(2)}) copy-start(bf16[2,512,256]{1,2,0:T(8,128)(2,1)S(1)} %get-tuple-element.135) | copy-start | bytes 1572868
  240.9 217.7 %all-gather.11.cloned.1.call-start = ((), (), s32[]{:S(2)}) async-start(), calls=%async_computation.15 | async-start | bytes 35651584 | tf_op jit(solution)/shard_map/all_gather | solution.py:182
  241.5 349.0 %all-gather.13.cloned.1.call-start = ((), (), s32[]{:S(2)}) async-start(), calls=%async_computation.16 | async-start | bytes 17825792 | tf_op jit(solution)/shard_map/all_gather | solution.py:183
  242.1 416.9 %all-reduce.16.cloned.1.call-start = ((), (), s32[]{:S(2)}) async-start(), calls=%async_computation.17 | async-start | bytes 2097152 | tf_op jit(solution)/shard_map/psum | solution.py:229
  666.8 19.1 %all-to-all-start.4 = ((bf16[256,4,256]{0,2,1:T(8,128)(2,1)}), bf16[256,4,256]{0,2,1:T(8,128)(2,1)S(1)}, u32[]{:S(2)}, u32[]{:S(2)}) async-start(bf16[256,4,256]{0,2,1:T(8,128)(2,1)} %bitcast.280), calls=%async_computation.4 | async-start | bytes 1048576 | tf_op jit(solution)/shard_map/all_to_all | solution.py:241
  718.2 5.1 copy-start.23
  719.8 17.5 %all-to-all-start.7 = ((bf16[4,256,256]{1,2,0:T(8,128)(2,1)}), bf16[4,256,256]{1,2,0:T(8,128)(2,1)S(1)}, u32[]{:S(2)}, u32[]{:S(2)}) async-start(bf16[4,256,256]{1,2,0:T(8,128)(2,1)} %copy.98), calls=%async_computation.7 | async-start | bytes 1048576 | tf_op jit(solution)/shard_map/all_to_all | solution.py:250
  737.3 5.6 copy-start.10
  737.3 18.7 %all-to-all-start.5 = ((bf16[4,256,256]{1,2,0:T(8,128)(2,1)}), bf16[4,256,256]{1,2,0:T(8,128)(2,1)}, u32[]{:S(2)}, u32[]{:S(2)}) async-start(bf16[4,256,256]{1,2,0:T(8,128)(2,1)} %copy.94), calls=%async_computation.5 | async-start | bytes 1048576 | tf_op jit(solution)/shard_map/all_to_all | solution.py:248
  744.3 15.9 copy-start.9
  756.0 18.3 %all-to-all-start.6 = ((bf16[4,256,256]{1,2,0:T(8,128)(2,1)}), bf16[4,256,256]{1,2,0:T(8,128)(2,1)}, u32[]{:S(2)}, u32[]{:S(2)}) async-start(bf16[4,256,256]{1,2,0:T(8,128)(2,1)} %copy.96), calls=%async_computation.6 | async-start | bytes 1048576 | tf_op jit(solution)/shard_map/all_to_all | solution.py:249
  760.1 254.8 %all-reduce.18.cloned.1.call-start = ((), (), s32[]{:S(2)}) async-start(), calls=%async_computation.22 | async-start | bytes 4194304 | tf_op jit(solution)/shard_map/psum | solution.py:213
  769.4 6.0 copy-start.27
  769.4 6.0 copy-start.28
  770.7 5.6 copy-start.18
  786.6 269.8 %reduce-scatter.15.cloned.1.call-start = ((), (), s32[]{:S(2)}) async-start(), calls=%async_computation.19 | async-start | bytes 4456448
  799.5 264.0 %reduce-scatter.13.cloned.1.call-start = ((), (), s32[]{:S(2)}) async-start(), calls=%async_computation.18 | async-start | bytes 13369344
  851.6 392.5 %reduce-scatter.19.cloned.1.call-start = ((), (), s32[]{:S(2)}) async-start(), calls=%async_computation.21 | async-start | bytes 17825792
  883.5 694.7 %reduce-scatter.17.cloned.1.call-start = ((), (), s32[]{:S(2)}) async-start(), calls=%async_computation.20 | async-start | bytes 35651584
  1013.1 38.2 %copy-start.33 = (f32[256]{0:T(256)S(1)}, f32[256]{0:T(256)}, u32[]{:S(2)}) copy-start(f32[256]{0:T(256)} %get-tuple-element.334) | copy-start | bytes 3076
  (32 other events, 62.6 us)
Sparse Core Ops, SparseCore 0:
  10.2 103.2 all-gather.6
  115.6 67.4 all-gather.8
  241.0 38.2 all-reduce.13
  280.7 177.8 all-gather.10
  460.5 129.8 all-gather.12
  620.7 38.2 all-reduce.15
  786.7 61.1 all-reduce.17
  851.7 72.7 reduce-scatter.14
  928.6 134.9 reduce-scatter.12
  1067.5 176.5 reduce-scatter.18
  1248.4 329.7 reduce-scatter.16
where the time goes:
time: 1610 us; the launch traced here: 1600 us
  waiting for transfers between devices  996 us (62%)
  local copies, waits for them, and re-layouts  256 us (16%)
  matrix products  148 us (9%)
  blocking collectives  116 us (7%)
  other arithmetic  37.1 us (2%)
  starting transfers between devices  29.3 us (2%)
    unnamed x15, waiting for transfers between devices  514 us
    unnamed x70, local copies, waits for them, and re-layouts  211 us
    all_gather x1, waiting for transfers between devices, on_device(): lax.all_gather(w_gate_up, ('shard', 'ctx'), axis=1, tiled=True)  178 us
    dot_general x24, matrix products, contract(): jnp.einsum(form, left_in, right_in, preferred_element_type=jnp.float32)  134 us
    all_gather x1, waiting for transfers between devices, on_device(): lax.all_gather(w_down, ('shard', 'ctx'), axis=1, tiled=True)  114 us
    all_gather x1, waiting for transfers between devices, on_device(): lax.all_gather(w_qkv, ('shard', 'ctx'), axis=1, tiled=True)  66.9 us
    psum x1, waiting for transfers between devices, on_device(): lax.psum(terms_two.astype(jnp.bfloat16), 'tp').astype(jnp.float32)  38.4 us
    all_gather x1, blocking collectives, on_device(): lax.all_gather(gain_attn, ('shard', 'ctx'), axis=0, tiled=True)  35 us
  transfers between devices with their start and end apart: 18, of which 15 were waited for; matrix products, arithmetic and copies ran while one was open for 21% of the time, Pallas kernels for 0%

commit v1 on v0

--- a/solution.py
+++ b/solution.py
@@ -7,6 +7,23 @@
 EPSILON = 1e-05
 ROPE_BASE = 130000.0
 MASKED = -1e30
+
+
+def laid_out(tiles, dim):
+    tiles = jnp.moveaxis(tiles, 0, dim)
+    dims = tiles.shape
+    return tiles.reshape(*dims[:dim], dims[dim] * dims[dim + 1], *dims[dim + 2 :])
+
+
+def gather_around(shard, axis, dim):
+    devices = lax.axis_size(axis)
+    right = [(i, (i + 1) % devices) for i in range(devices)]
+    blocks = [shard]
+    while len(blocks) < devices:
+        blocks.append(lax.ppermute(blocks[-1], axis, right))
+    index = lax.axis_index(axis)
+    blocks = jnp.stack(blocks)[(index - jnp.arange(devices)) % devices]
+    return laid_out(blocks, dim)
 
 
 def contract(form, left_in, right_in):
@@ -180,7 +197,7 @@
         lax.all_gather(w_out, ("shard", "ctx"), axis=1, tiled=True),
         lax.all_gather(gain_mlp, ("shard", "ctx"), axis=0, tiled=True),
         lax.all_gather(w_gate_up, ("shard", "ctx"), axis=1, tiled=True),
-        lax.all_gather(w_down, ("shard", "ctx"), axis=1, tiled=True),
+        gather_around(w_down, ("shard", "ctx"), 1),
     )
     gain_full_one, qkv_full, out_full, gain_full_two, gate_up_full, down_full = gathered
     resid_in = hidden_in.astype(jnp.float32)

time: 1610 us -> 1900 us (1.18)
  waiting for transfers between devices: 996 us -> 1190 us
  local copies, waits for them, and re-layouts: 256 us -> 307 us
  blocking collectives: 116 us -> 145 us
    ppermute x0 -> x15, waiting for transfers between devices: none -> 365 us  [gather_around(): blocks.append(lax.ppermute(blocks[-1], axis, right))]
    all_gather x1, waiting for transfers between devices: 178 us -> 0.02 us  [on_device(): lax.all_gather(w_gate_up, ('shard', 'ctx'), axis=1, tiled=True)]
    all_gather x1, blocking collectives: 28.8 us -> 59.5 us  [on_device(): lax.all_gather(gain_mlp, ('shard', 'ctx'), axis=0, tiled=True)]
    unnamed x70 -> x81, local copies, waits for them, and re-layouts: 211 us -> 235 us
    transpose x0 -> x1, local copies, waits for them, and re-layouts: none -> 20.7 us  [laid_out(): tiles = jnp.moveaxis(tiles, 0, dim)]
  transfers between devices with their start and end apart: 18 -> 33, of which waited for: 15 -> 22; matrix products, arithmetic and copies ran while one was open for 21% -> 25% of each run, Pallas kernels for 0% -> 0%
where the time goes in v1:
time: 1900 us; the launch traced here: 1890 us
  waiting for transfers between devices  1190 us (63%)
  local copies, waits for them, and re-layouts  307 us (16%)
  matrix products  163 us (9%)
  blocking collectives  145 us (8%)
  other arithmetic  34.5 us (2%)
  starting transfers between devices  34.4 us (2%)
    unnamed x15, waiting for transfers between devices  512 us
    ppermute x15, waiting for transfers between devices, gather_around(): blocks.append(lax.ppermute(blocks[-1], axis, right))  365 us
    unnamed x81, local copies, waits for them, and re-layouts  235 us
    dot_general x24, matrix products, contract(): jnp.einsum(form, left_in, right_in, preferred_element_type=jnp.float32)  139 us
    all_gather x1, waiting for transfers between devices, on_device(): lax.all_gather(w_down, ('shard', 'ctx'), axis=1, tiled=True)  121 us
    all_gather x1, waiting for transfers between devices, on_device(): lax.all_gather(w_qkv, ('shard', 'ctx'), axis=1, tiled=True)  66.2 us
    all_gather x1, blocking collectives, on_device(): lax.all_gather(gain_mlp, ('shard', 'ctx'), axis=0, tiled=True)  59.5 us
  transfers between devices with their start and end apart: 33, of which 22 were waited for; matrix products, arithmetic and copies ran while one was open for 25% of the time, Pallas kernels for 0%

profile of v1, /device:TPU:0, one launch (start us, length us, event | category | flops | bytes accessed | tf_op | source)
XLA Modules:
  0.0 1887.8 jit_solution(12613524223437182166)
XLA Ops:
  8.7 35.0 %all-gather = bf16[16,1,128]{2,1,0:T(2,128)(2,1)S(1)} all-gather(bf16[1,1,128]{2,1,0:T(2,128)(2,1)} %bitcast.372), channel_id=1, replica_groups=mesh['shard'=4,'ctx'=4,'tp'=2] {'shard','ctx'}, dimensions={0}, use_global_device_ids=true | all-gather | bytes 4352 | tf_op jit(solution)/shard_map/all_gather | solution.py:195
  47.4 66.2 %all-gather.7.cloned.1.call-done = bf16[3,2048,1024]{2,1,0:T(8,128)(2,1)} async-done(((bf16[3,128,1024]{2,1,0:T(8,128)(2,1)}), bf16[3,2048,1024]{2,1,0:T(8,128)(2,1)}) %all-gather.7.cloned.1.call-update) | async-done | bytes 12582928 | tf_op jit(solution)/shard_map/all_gather | solution.py:196
  152.1 26.6 %all-to-all-done.2 = bf16[256,4,256]{0,2,1:T(8,128)(2,1)S(1)} async-done(((bf16[256,4,256]{0,2,1:T(8,128)(2,1)}), bf16[256,4,256]{0,2,1:T(8,128)(2,1)S(1)}, u32[]{:S(2)}, u32[]{:S(2)}) %all-to-all-start.2) | async-done | bytes 524320 | tf_op jit(solution)/shard_map/all_to_all | solution.py:213
  214.8 16.7 all_to_all.107
  237.9 26.4 %collective-permute-done = bf16[4096,128]{1,0:T(8,128)(2,1)S(1)} collective-permute-done((bf16[4096,128]{1,0:T(8,128)(2,1)}, bf16[4096,128]{1,0:T(8,128)(2,1)S(1)}, u32[]{:S(2)}, u32[]{:S(2)}) %collective-permute-start) | collective-permute-done | bytes 1048608 | tf_op jit(solution)/shard_map/ppermute | solution.py:23
  264.3 27.6 %collective-permute-done.1 = bf16[4096,128]{1,0:T(8,128)(2,1)S(1)} collective-permute-done((bf16[4096,128]{1,0:T(8,128)(2,1)S(1)}, bf16[4096,128]{1,0:T(8,128)(2,1)S(1)}, u32[]{:S(2)}, u32[]{:S(2)}) %collective-permute-start.1) | collective-permute-done | bytes 1048608 | tf_op jit(solution)/shard_map/ppermute | solution.py:23
  291.9 37.1 %collective-permute-done.2 = bf16[4096,128]{1,0:T(8,128)(2,1)S(1)} collective-permute-done((bf16[4096,128]{1,0:T(8,128)(2,1)S(1)}, bf16[4096,128]{1,0:T(8,128)(2,1)S(1)}, u32[]{:S(2)}, u32[]{:S(2)}) %collective-permute-start.2) | collective-permute-done | bytes 1048608 | tf_op jit(solution)/shard_map/ppermute | solution.py:23
  329.9 36.9 %collective-permute-done.3 = bf16[4096,128]{1,0:T(8,128)(2,1)S(1)} collective-permute-done((bf16[4096,128]{1,0:T(8,128)(2,1)S(1)}, bf16[4096,128]{1,0:T(8,128)(2,1)S(1)}, u32[]{:S(2)}, u32[]{:S(2)}) %collective-permute-start.3) | collective-permute-done | bytes 1048608 | tf_op jit(solution)/shard_map/ppermute | solution.py:23
  367.8 35.6 %collective-permute-done.4 = bf16[4096,128]{1,0:T(8,128)(2,1)} collective-permute-done((bf16[4096,128]{1,0:T(8,128)(2,1)S(1)}, bf16[4096,128]{1,0:T(8,128)(2,1)}, u32[]{:S(2)}, u32[]{:S(2)}) %collective-permute-start.4) | collective-permute-done | bytes 1048608 | tf_op jit(solution)/shard_map/ppermute | solution.py:23
  403.4 59.5 %all-gather.1 = bf16[16,1,128]{2,1,0:T(2,128)(2,1)S(1)} all-gather(bf16[1,1,128]{2,1,0:T(2,128)(2,1)S(1)} %bitcast.373), channel_id=1, replica_groups=mesh['shard'=4,'ctx'=4,'tp'=2] {'shard','ctx'}, dimensions={0}, use_global_device_ids=true | all-gather | bytes 4352 | tf_op jit(solution)/shard_map/all_gather | solution.py:198
  467.6 33.9 %collective-permute-done.6 = bf16[4096,128]{1,0:T(8,128)(2,1)S(1)} collective-permute-done((bf16[4096,128]{1,0:T(8,128)(2,1)}, bf16[4096,128]{1,0:T(8,128)(2,1)S(1)}, u32[]{:S(2)}, u32[]{:S(2)}) %collective-permute-start.6) | collective-permute-done | bytes 1048608 | tf_op jit(solution)/shard_map/ppermute | solution.py:23
  503.6 36.0 %collective-permute-done.7 = bf16[4096,128]{1,0:T(8,128)(2,1)S(1)} collective-permute-done((bf16[4096,128]{1,0:T(8,128)(2,1)S(1)}, bf16[4096,128]{1,0:T(8,128)(2,1)S(1)}, u32[]{:S(2)}, u32[]{:S(2)}) %collective-permute-start.7) | collective-permute-done | bytes 1048608 | tf_op jit(solution)/shard_map/ppermute | solution.py:23
  541.7 35.7 %collective-permute-done.8 = bf16[4096,128]{1,0:T(8,128)(2,1)S(1)} collective-permute-done((bf16[4096,128]{1,0:T(8,128)(2,1)S(1)}, bf16[4096,128]{1,0:T(8,128)(2,1)S(1)}, u32[]{:S(2)}, u32[]{:S(2)}) %collective-permute-start.8) | collective-permute-done | bytes 1048608 | tf_op jit(solution)/shard_map/ppermute | solution.py:23
  582.0 32.9 %collective-permute-done.9 = bf16[4096,128]{1,0:T(8,128)(2,1)S(1)} collective-permute-done((bf16[4096,128]{1,0:T(8,128)(2,1)S(1)}, bf16[4096,128]{1,0:T(8,128)(2,1)S(1)}, u32[]{:S(2)}, u32[]{:S(2)}) %collective-permute-start.9) | collective-permute-done | bytes 1048608 | tf_op jit(solution)/shard_map/ppermute | solution.py:23
  617.2 35.1 %collective-permute-done.10 = bf16[4096,128]{1,0:T(8,128)(2,1)S(1)} collective-permute-done((bf16[4096,128]{1,0:T(8,128)(2,1)S(1)}, bf16[4096,128]{1,0:T(8,128)(2,1)S(1)}, u32[]{:S(2)}, u32[]{:S(2)}) %collective-permute-start.10) | collective-permute-done | bytes 1048608 | tf_op jit(solution)/shard_map/ppermute | solution.py:23
  655.4 28.2 %collective-permute-done.11 = bf16[4096,128]{1,0:T(8,128)(2,1)} collective-permute-done((bf16[4096,128]{1,0:T(8,128)(2,1)S(1)}, bf16[4096,128]{1,0:T(8,128)(2,1)}, u32[]{:S(2)}, u32[]{:S(2)}) %collective-permute-start.11) | collective-permute-done | bytes 1048608 | tf_op jit(solution)/shard_map/ppermute | solution.py:23
  685.4 17.4 convolution_bitcast_fusion
  702.8 120.8 %all-gather.13.cloned.1.call-done = bf16[4096,2048]{1,0:T(8,128)(2,1)} async-done(((bf16[4096,128]{1,0:T(8,128)(2,1)}), bf16[4096,2048]{1,0:T(8,128)(2,1)}) %all-gather.13.cloned.1.call-update) | async-done | bytes 16777232 | tf_op jit(solution)/shard_map/all_gather | solution.py:236
  836.5 16.7 fusion.63
  857.8 33.8 %all-reduce.16.cloned.1.call-done = bf16[256,2048]{1,0:T(8,128)(2,1)} async-done(((bf16[256,2048]{1,0:T(8,128)(2,1)}), bf16[256,2048]{1,0:T(8,128)(2,1)}) %all-reduce.16.cloned.1.call-update) | async-done | bytes 1048592 | tf_op jit(solution)/shard_map/psum | solution.py:246
  909.3 32.3 %all-to-all-done.4 = bf16[256,4,256]{0,2,1:T(8,128)(2,1)S(1)} async-done(((bf16[256,4,256]{0,2,1:T(8,128)(2,1)}), bf16[256,4,256]{0,2,1:T(8,128)(2,1)S(1)}, u32[]{:S(2)}, u32[]{:S(2)}) %all-to-all-start.4) | async-done | bytes 524320 | tf_op jit(solution)/shard_map/all_to_all | solution.py:258
  946.6 24.8 %while.27 = (s32[]{:T(128)}, bf16[2,512,4,64]{1,3,2,0:T(8,128)(2,1)}, f32[2,1024,4,64]{1,3,2,0:T(8,128)}, f32[2,1024,4,64]{1,3,2,0:T(8,128)}, bf16[2,1024,4,64]{...) while((s32[]{:T(128)}, ...), condition=%wide.region_14.15_spmd, body=%wide.region_12.14_spmd.sunk | while | flops 1365637120 | bytes 89220488 | solution.py:158
  1012.2 20.7 %copy.90 = bf16[4096,16,128]{0,2,1:T(8,128)(2,1)} copy(bf16[4096,16,128]{2,0,1:T(8,128)(2,1)} %bitcast.326) | data formatting | bytes 33554432 | tf_op jit(solution)/shard_map/transpose | solution.py:13
  1042.0 19.1 %convolution_convert_fusion.2 = bf16[256,2048]{1,0:T(8,128)(2,1)} fusion(bf16[4096,2048]{0,1:T(8,128)(2,1)} %bitcast.328, f32[2,256,4096]{2,1,0:T(8,128)} %convolution_bitcast_fusion), kind=kOutput, calls=%fused_computation.105 | convolution fusion | flops 4301783040 | bytes 26214400 | tf_op jit(solution)/shard_map/dot_general | solution.py:228
  1094.9 27.7 %copy.113 = bf16[3,2048,1024]{2,0,1:T(4,128)(2,1)} copy(bf16[3,2048,1024]{1,2,0:T(8,128)(2,1)} %convert_bitcast_fusion.1) | data formatting | bytes 25165824
  1153.4 21.7 %copy.119 = bf16[4096,2048]{0,1:T(8,128)(2,1)} copy(bf16[4096,2048]{1,0:T(8,128)(2,1)} %convolution_convert_fusion) | data formatting | bytes 33554432
  1175.4 16.4 convert_bitcast_fusion
  1191.8 83.2 %copy.117 = bf16[2,2048,4096]{2,0,1:T(2,128)(2,1)} copy(bf16[2,2048,4096]{1,2,0:T(8,128)(2,1)} %convert_bitcast_fusion) | data formatting | bytes 67108864
  1275.0 29.5 %copy.122 = bf16[256,8,2,4096]{3,1,2,0:T(8,128)(2,1)} copy(bf16[256,8,2,4096]{3,2,1,0:T(2,128)(2,1)} %bitcast.323) | data formatting | bytes 67108864
  1308.3 34.2 %all-reduce.8 = (bf16[2048]{0:T(1024)(128)(2,1)S(1)}, bf16[2048]{0:T(1024)(128)(2,1)S(1)}) all-reduce(bf16[2048]{0:T(1024)(128)(2,1)S(1)} %get-tuple-element.246, bf16[2048]{0:T(1024)(128)(2,1)S(1)} %copy-done.30), channel_id=2, replica_groups=mesh['shard'=4,'ctx'=4,'tp'=2] {'shard','ctx'}, use_global_device_ids=true, to_apply=%region_18.19.clone | all-reduce | flops 4096 | bytes 16384
  1359.2 175.2 %reduce-scatter.19.cloned.1.call-done = bf16[128,4096]{1,0:T(8,128)(2,1)} async-done(((bf16[2048,4096]{1,0:T(8,128)(2,1)}), bf16[128,4096]{1,0:T(8,128)(2,1)}) %reduce-scatter.19.cloned.1.call-update) | async-done | bytes 1048592
  1537.5 330.9 %reduce-scatter.17.cloned.1.call-done = bf16[128,8192]{1,0:T(8,128)(2,1)} async-done(((bf16[2048,8192]{1,0:T(8,128)(2,1)}), bf16[128,8192]{1,0:T(8,128)(2,1)}) %reduce-scatter.17.cloned.1.call-update) | async-done | bytes 2097168
  (309 shorter events, 336.9 us)
Async XLA Ops:
  7.2 106.3 %all-gather.7.cloned.1.call-start = ((), (), s32[]{:S(2)}) async-start(), calls=%async_computation.12 | async-start | bytes 13369344 | tf_op jit(solution)/shard_map/all_gather | solution.py:196
  7.9 223.8 %all-gather.9.cloned.1.call-start = ((), (), s32[]{:S(2)}) async-start(), calls=%async_computation.13 | async-start | bytes 4456448 | tf_op jit(solution)/shard_map/all_gather | solution.py:197
  123.3 24.4 %all-to-all-start = ((bf16[256,4,256]{0,2,1:T(8,128)(2,1)}), bf16[256,4,256]{0,2,1:T(8,128)(2,1)}, u32[]{:S(2)}, u32[]{:S(2)}) async-start(bf16[256,4,256]{0,2,1:T(8,128)(2,1)} %bitcast.344), calls=%async_computation | async-start | bytes 1048576 | tf_op jit(solution)/shard_map/all_to_all | solution.py:214
  147.8 30.9 %all-to-all-start.2 = ((bf16[256,4,256]{0,2,1:T(8,128)(2,1)}), bf16[256,4,256]{0,2,1:T(8,128)(2,1)S(1)}, u32[]{:S(2)}, u32[]{:S(2)}) async-start(bf16[256,4,256]{0,2,1:T(8,128)(2,1)} %bitcast.39), calls=%async_computation.2 | async-start | bytes 1048576 | tf_op jit(solution)/shard_map/all_to_all | solution.py:213
  178.7 18.6 all-to-all-start.1
  182.2 501.4 %all-reduce.14.cloned.1.call-start = ((), (), s32[]{:S(2)}) async-start(), calls=%async_computation.14 | async-start | bytes 2097152 | tf_op jit(solution)/shard_map/psum | solution.py:220
  236.4 449.0 %all-gather.11.cloned.1.call-start = ((), (), s32[]{:S(2)}) async-start(), calls=%async_computation.15 | async-start | bytes 35651584 | tf_op jit(solution)/shard_map/all_gather | solution.py:199
  237.0 586.6 %all-gather.13.cloned.1.call-start = ((), (), s32[]{:S(2)}) async-start(), calls=%async_computation.16 | async-start | bytes 17825792 | tf_op jit(solution)/shard_map/all_gather | solution.py:236
  237.5 654.1 %all-reduce.16.cloned.1.call-start = ((), (), s32[]{:S(2)}) async-start(), calls=%async_computation.17 | async-start | bytes 2097152 | tf_op jit(solution)/shard_map/psum | solution.py:246
  237.6 26.7 %collective-permute-start = (bf16[4096,128]{1,0:T(8,128)(2,1)}, bf16[4096,128]{1,0:T(8,128)(2,1)S(1)}, u32[]{:S(2)}, u32[]{:S(2)}) collective-permute-start(bf16[4096,128]{1,0:T(8,128)(2,1)} %param.19), channel_id=1, source_target_pairs={{0,2},{2,4},{4,6},{6,8},{8,10},{10,12},{12,14},{14,16},{16,18},{18... | collective-permute-start | bytes 3145736 | tf_op jit(solution)/shard_map/ppermute | solution.py:23
  264.3 27.6 %collective-permute-start.1 = (bf16[4096,128]{1,0:T(8,128)(2,1)S(1)}, bf16[4096,128]{1,0:T(8,128)(2,1)S(1)}, u32[]{:S(2)}, u32[]{:S(2)}) collective-permute-start(bf16[4096,128]{1,0:T(8,128)(2,1)S(1)} %collective-permute-done), channel_id=1, source_target_pairs={{0,2},{2,4},{4,6},{6,8},{8,10},{10,12},{12,14},{14,16},{16,18},{18... | collective-permute-start | bytes 3145736 | tf_op jit(solution)/shard_map/ppermute | solution.py:23
  291.9 37.1 %collective-permute-start.2 = (bf16[4096,128]{1,0:T(8,128)(2,1)S(1)}, bf16[4096,128]{1,0:T(8,128)(2,1)S(1)}, u32[]{:S(2)}, u32[]{:S(2)}) collective-permute-start(bf16[4096,128]{1,0:T(8,128)(2,1)S(1)} %collective-permute-done.1), channel_id=1, source_target_pairs={{0,2},{2,4},{4,6},{6,8},{8,10},{10,12},{12,14},{14,16},{16,18},{18... | collective-permute-start | bytes 3145736 | tf_op jit(solution)/shard_map/ppermute | solution.py:23
  329.9 36.9 %collective-permute-start.3 = (bf16[4096,128]{1,0:T(8,128)(2,1)S(1)}, bf16[4096,128]{1,0:T(8,128)(2,1)S(1)}, u32[]{:S(2)}, u32[]{:S(2)}) collective-permute-start(bf16[4096,128]{1,0:T(8,128)(2,1)S(1)} %collective-permute-done.2), channel_id=1, source_target_pairs={{0,2},{2,4},{4,6},{6,8},{8,10},{10,12},{12,14},{14,16},{16,18},{18... | collective-permute-start | bytes 3145736 | tf_op jit(solution)/shard_map/ppermute | solution.py:23
  366.8 36.6 %collective-permute-start.4 = (bf16[4096,128]{1,0:T(8,128)(2,1)S(1)}, bf16[4096,128]{1,0:T(8,128)(2,1)}, u32[]{:S(2)}, u32[]{:S(2)}) collective-permute-start(bf16[4096,128]{1,0:T(8,128)(2,1)S(1)} %collective-permute-done.3), channel_id=1, source_target_pairs={{0,2},{2,4},{4,6},{6,8},{8,10},{10,12},{12,14},{14,16},{16,18},{18... | collective-permute-start | bytes 3145736 | tf_op jit(solution)/shard_map/ppermute | solution.py:23
  403.4 59.5 %collective-permute-start.5 = (bf16[4096,128]{1,0:T(8,128)(2,1)}, bf16[4096,128]{1,0:T(8,128)(2,1)}, u32[]{:S(2)}, u32[]{:S(2)}) collective-permute-start(bf16[4096,128]{1,0:T(8,128)(2,1)} %collective-permute-done.4), channel_id=1, source_target_pairs={{0,2},{2,4},{4,6},{6,8},{8,10},{10,12},{12,14},{14,16},{16,18},{18... | collective-permute-start | bytes 3145736 | tf_op jit(solution)/shard_map/ppermute | solution.py:23
  462.9 38.6 %collective-permute-start.6 = (bf16[4096,128]{1,0:T(8,128)(2,1)}, bf16[4096,128]{1,0:T(8,128)(2,1)S(1)}, u32[]{:S(2)}, u32[]{:S(2)}) collective-permute-start(bf16[4096,128]{1,0:T(8,128)(2,1)} %collective-permute-done.5), channel_id=1, source_target_pairs={{0,2},{2,4},{4,6},{6,8},{8,10},{10,12},{12,14},{14,16},{16,18},{18... | collective-permute-start | bytes 3145736 | tf_op jit(solution)/shard_map/ppermute | solution.py:23
  501.5 38.1 %collective-permute-start.7 = (bf16[4096,128]{1,0:T(8,128)(2,1)S(1)}, bf16[4096,128]{1,0:T(8,128)(2,1)S(1)}, u32[]{:S(2)}, u32[]{:S(2)}) collective-permute-start(bf16[4096,128]{1,0:T(8,128)(2,1)S(1)} %collective-permute-done.6), channel_id=1, source_target_pairs={{0,2},{2,4},{4,6},{6,8},{8,10},{10,12},{12,14},{14,16},{16,18},{18... | collective-permute-start | bytes 3145736 | tf_op jit(solution)/shard_map/ppermute | solution.py:23
  539.6 37.8 %collective-permute-start.8 = (bf16[4096,128]{1,0:T(8,128)(2,1)S(1)}, bf16[4096,128]{1,0:T(8,128)(2,1)S(1)}, u32[]{:S(2)}, u32[]{:S(2)}) collective-permute-start(bf16[4096,128]{1,0:T(8,128)(2,1)S(1)} %collective-permute-done.7), channel_id=1, source_target_pairs={{0,2},{2,4},{4,6},{6,8},{8,10},{10,12},{12,14},{14,16},{16,18},{18... | collective-permute-start | bytes 3145736 | tf_op jit(solution)/shard_map/ppermute | solution.py:23
  577.4 37.5 %collective-permute-start.9 = (bf16[4096,128]{1,0:T(8,128)(2,1)S(1)}, bf16[4096,128]{1,0:T(8,128)(2,1)S(1)}, u32[]{:S(2)}, u32[]{:S(2)}) collective-permute-start(bf16[4096,128]{1,0:T(8,128)(2,1)S(1)} %collective-permute-done.8), channel_id=1, source_target_pairs={{0,2},{2,4},{4,6},{6,8},{8,10},{10,12},{12,14},{14,16},{16,18},{18... | collective-permute-start | bytes 3145736 | tf_op jit(solution)/shard_map/ppermute | solution.py:23
  614.9 37.4 %collective-permute-start.10 = (bf16[4096,128]{1,0:T(8,128)(2,1)S(1)}, bf16[4096,128]{1,0:T(8,128)(2,1)S(1)}, u32[]{:S(2)}, u32[]{:S(2)}) collective-permute-start(bf16[4096,128]{1,0:T(8,128)(2,1)S(1)} %collective-permute-done.9), channel_id=1, source_target_pairs={{0,2},{2,4},{4,6},{6,8},{8,10},{10,12},{12,14},{14,16},{16,18},{18... | collective-permute-start | bytes 3145736 | tf_op jit(solution)/shard_map/ppermute | solution.py:23
  653.3 30.3 %collective-permute-start.11 = (bf16[4096,128]{1,0:T(8,128)(2,1)S(1)}, bf16[4096,128]{1,0:T(8,128)(2,1)}, u32[]{:S(2)}, u32[]{:S(2)}) collective-permute-start(bf16[4096,128]{1,0:T(8,128)(2,1)S(1)} %collective-permute-done.10), channel_id=1, source_target_pairs={{0,2},{2,4},{4,6},{6,8},{8,10},{10,12},{12,14},{14,16},{16,18},{18... | collective-permute-start | bytes 3145736 | tf_op jit(solution)/shard_map/ppermute | solution.py:23
  683.6 174.2 %collective-permute-start.12 = (bf16[4096,128]{1,0:T(8,128)(2,1)}, bf16[4096,128]{1,0:T(8,128)(2,1)}, u32[]{:S(2)}, u32[]{:S(2)}) collective-permute-start(bf16[4096,128]{1,0:T(8,128)(2,1)} %collective-permute-done.11), channel_id=1, source_target_pairs={{0,2},{2,4},{4,6},{6,8},{8,10},{10,12},{12,14},{14,16},{16,18},{18... | collective-permute-start | bytes 3145736 | tf_op jit(solution)/shard_map/ppermute | solution.py:23
  857.8 49.3 %collective-permute-start.13 = (bf16[4096,128]{1,0:T(8,128)(2,1)}, bf16[4096,128]{1,0:T(8,128)(2,1)}, u32[]{:S(2)}, u32[]{:S(2)}) collective-permute-start(bf16[4096,128]{1,0:T(8,128)(2,1)} %collective-permute-done.12), channel_id=1, source_target_pairs={{0,2},{2,4},{4,6},{6,8},{8,10},{10,12},{12,14},{14,16},{16,18},{18... | collective-permute-start | bytes 3145736 | tf_op jit(solution)/shard_map/ppermute | solution.py:23
  900.2 41.4 %all-to-all-start.4 = ((bf16[256,4,256]{0,2,1:T(8,128)(2,1)}), bf16[256,4,256]{0,2,1:T(8,128)(2,1)S(1)}, u32[]{:S(2)}, u32[]{:S(2)}) async-start(bf16[256,4,256]{0,2,1:T(8,128)(2,1)} %bitcast.346), calls=%async_computation.4 | async-start | bytes 1048576 | tf_op jit(solution)/shard_map/all_to_all | solution.py:258
  907.1 89.7 %collective-permute-start.14 = (bf16[4096,128]{1,0:T(8,128)(2,1)}, bf16[4096,128]{1,0:T(8,128)(2,1)}, u32[]{:S(2)}, u32[]{:S(2)}) collective-permute-start(bf16[4096,128]{1,0:T(8,128)(2,1)} %collective-permute-done.13), channel_id=1, source_target_pairs={{0,2},{2,4},{4,6},{6,8},{8,10},{10,12},{12,14},{14,16},{16,18},{18... | collective-permute-start | bytes 3145736 | tf_op jit(solution)/shard_map/ppermute | solution.py:23
  992.9 44.0 %all-to-all-start.5 = ((bf16[4,256,256]{1,2,0:T(8,128)(2,1)}), bf16[4,256,256]{1,2,0:T(8,128)(2,1)S(1)}, u32[]{:S(2)}, u32[]{:S(2)}) async-start(bf16[4,256,256]{1,2,0:T(8,128)(2,1)} %copy.96), calls=%async_computation.5 | async-start | bytes 1048576 | tf_op jit(solution)/shard_map/all_to_all | solution.py:265
  1036.9 25.3 %all-to-all-start.6 = ((bf16[4,256,256]{1,2,0:T(8,128)(2,1)}), bf16[4,256,256]{1,2,0:T(8,128)(2,1)S(1)}, u32[]{:S(2)}, u32[]{:S(2)}) async-start(bf16[4,256,256]{1,2,0:T(8,128)(2,1)} %copy.98), calls=%async_computation.6 | async-start | bytes 1048576 | tf_op jit(solution)/shard_map/all_to_all | solution.py:266
  1042.0 264.5 %all-reduce.18.cloned.1.call-start = ((), (), s32[]{:S(2)}) async-start(), calls=%async_computation.22 | async-start | bytes 4194304 | tf_op jit(solution)/shard_map/psum | solution.py:230
  1074.4 274.5 %reduce-scatter.15.cloned.1.call-start = ((), (), s32[]{:S(2)}) async-start(), calls=%async_computation.19 | async-start | bytes 4456448
  1086.2 268.0 %reduce-scatter.13.cloned.1.call-start = ((), (), s32[]{:S(2)}) async-start(), calls=%async_computation.18 | async-start | bytes 13369344
  1138.5 396.0 %reduce-scatter.19.cloned.1.call-start = ((), (), s32[]{:S(2)}) async-start(), calls=%async_computation.21 | async-start | bytes 17825792
  1175.1 693.3 %reduce-scatter.17.cloned.1.call-start = ((), (), s32[]{:S(2)}) async-start(), calls=%async_computation.20 | async-start | bytes 35651584
  (45 other events, 1082.4 us)
Sparse Core Ops, SparseCore 0:
  10.2 103.2 all-gather.6
  115.6 67.7 all-gather.8
  236.5 38.6 all-reduce.13
  276.6 397.7 all-gather.10
  676.3 147.2 all-gather.12
  853.3 38.2 all-reduce.15
  1074.5 63.4 all-reduce.17
  1141.9 72.8 reduce-scatter.14
  1218.8 135.3 reduce-scatter.12
  1358.2 176.2 reduce-scatter.18
  1538.7 329.7 reduce-scatter.16
